TPU v7x, 32 devices: a whole 2x2x4 slice. The times are simulated.
32 devices in a mesh: band: 16 (over z, x, core), fld: 2 (over y).
Axes of the slice: x: 2, y: 2, z: 4, core: 2. Of those that a mesh axis runs over, the one named last changes fastest.
Arguments:
- grid_field: bfloat16 [2, 4, 1280, 2, 5248], P(None, 'fld', 'band'), may hold values from -6 to 6
- coupling: float32 [2, 4], P(None, 'fld'), may hold values from 0.1 to 1
- points: int32 [1280], replicated, may hold values from 20 to 5136, as said below
- lat_ids: int32 [1280], P('band'), may hold values from 0 to 1279, each once
- wn_ids: int32 [128], P('band'), may hold values from 0 to 1279, as said below
Outputs:
- new_grid: bfloat16 [2, 4, 1280, 2, 5248], P(None, 'fld', 'band')
Inputs may be any that keep to these rules, and one draw needn't show every extreme that they name: Latitude i has 20 + 4 i points or up to 8 fewer, a multiple of 4, never under 20; the last latitude has exactly the most. `lat_ids`: each hemispheric latitude stands in exactly one slot. `wn_ids`: distinct wavenumbers; 0 and 1279 are always among them.
All inputs are finite; a program needn't handle non-finite values.
Results may differ from a plain program's by a relative error of at most 0.014.
Values may be sent and summed in bfloat16 or wider, within the bound.
No kernel may reach another device: no remote copies, remote signals or barrier semaphores. Data moves between devices by JAX's collectives and lax.ppermute only.
A program may use at most 128 MiB of HBM per device.

v0:
```python
import math
import jax
import jax.numpy as jnp
from jax import lax
from jax.sharding import PartitionSpec as P

NT = 1279
NH = 1280
PPAD = 5248
rescale_limit = 2.0**60
rescale_log = 60.0 * math.log(2.0)


def carried_in(array, axis, join, neutral):
    place = lax.axis_index(axis)
    gathered = lax.all_gather(array.astype(jnp.bfloat16), axis)
    state = jnp.zeros_like(array) + jnp.asarray(neutral, array.dtype)

    def one(step, state):
        return join(state, lax.dynamic_index_in_dim(gathered, step, 0, False).astype(array.dtype))

    return lax.fori_loop(0, place, one, state)


def latitude_angles(lat_index):
    colatitude = math.pi * (lat_index.astype(jnp.float32) + 0.5) / (2.0 * NH)
    return (jnp.cos(colatitude), jnp.sin(colatitude))


def damping(orders):
    row_index = jnp.arange(NT + 1).astype(jnp.float32).reshape((NT + 1) // 2, 2)
    degree = row_index[:, :, None] + orders.astype(jnp.float32)[None, None, :]
    return 1.0 / (1.0 + 4.0 * degree * (degree + 1.0) / (NT * (NT + 1.0)))


def legendre_rows(orders, cosines, sines):
    order_f = orders.astype(jnp.float32)[:, None]
    step_index = jnp.arange(1, NT + 1).astype(jnp.float32)
    log_terms = jnp.log1p(0.5 / step_index)
    log_norm = 0.5 * math.log(0.5) + 0.5 * jnp.sum(
        jnp.where(step_index[None, :] <= order_f, log_terms[None, :], 0.0), axis=1
    )
    scaled_log = log_norm[:, None] + order_f * jnp.log(sines)[None, :]
    start_row = jnp.ones(scaled_log.shape, jnp.float32)
    cosine_row = cosines[None, :]
    offsets = jnp.arange(1, NT + 2).astype(jnp.float32)[:, None, None]
    degrees = order_f[None] + offsets
    factors = jnp.sqrt(
        (4.0 * degrees * degrees - 1.0) / (offsets * (2.0 * order_f[None] + offsets))
    )
    backwards = jnp.sqrt(
        (offsets - 1.0)
        * (2.0 * order_f[None] + offsets - 1.0)
        / (4.0 * (degrees - 1.0) * (degrees - 1.0) - 1.0)
    )
    inside_rows = degrees - 1.0 <= NT

    def advance(state_now, step_terms):
        current, previous, running_log = state_now
        factor, backward, inside = step_terms
        row_value = jnp.where(inside, current * jnp.exp(running_log), 0.0).astype(jnp.bfloat16)
        newest = factor * (cosine_row * current - backward * previous)
        oversize = jnp.abs(newest) > rescale_limit
        shrink = jnp.where(oversize, 1.0 / rescale_limit, 1.0)
        running_log = running_log + jnp.where(oversize, rescale_log, 0.0)
        newest = newest * shrink
        current = current * shrink
        return ((newest, current, running_log), row_value)

    final_state, every_row = lax.scan(
        advance,
        (start_row, jnp.zeros_like(start_row), scaled_log),
        (factors, backwards, inside_rows),
        unroll=8,
    )
    return every_row.reshape(((NT + 1) // 2, 2) + every_row.shape[1:])


def fourier_tables(counts, orders, blocks):
    inner_index = jnp.arange(128)
    block_start = jnp.arange(blocks) * 128
    periods = counts[:, None, None]
    inner_residue = inner_index[None, :, None] * orders[None, None, :] % periods
    block_residue = block_start[None, :, None] * orders[None, None, :] % periods
    period_f = periods.astype(jnp.float32)
    inner_angle = 2.0 * math.pi * inner_residue.astype(jnp.float32) / period_f
    block_angle = 2.0 * math.pi * block_residue.astype(jnp.float32) / period_f
    return (
        jnp.cos(inner_angle).astype(jnp.bfloat16),
        jnp.sin(inner_angle).astype(jnp.bfloat16),
        jnp.cos(block_angle),
        jnp.sin(block_angle),
    )


def analyse(grid_field, counts, orders, weights):
    blocks = PPAD // 128
    order_count = orders.shape[0]
    cos_inner, sin_inner, cos_outer, sin_outer = fourier_tables(counts, orders, blocks)
    inside = jnp.arange(PPAD)[None, :] < counts[:, None]
    masked = jnp.where(inside[:, None, :], grid_field, jnp.zeros((), jnp.bfloat16))
    shaped = masked.reshape(grid_field.shape[:-1] + (blocks, 128))
    dft_table = jnp.concatenate([cos_inner, -sin_inner], axis=-1)
    partial_sums = jnp.einsum(
        "vlshbk,skc->vlshbc", shaped, dft_table, preferred_element_type=jnp.float32
    )
    real_sums = partial_sums[..., :order_count]
    imag_sums = partial_sums[..., order_count:]
    outer_cos = cos_outer[:, None]
    outer_sin = sin_outer[:, None]
    period_f = counts.astype(jnp.float32)[:, None, None]
    real_coef = jnp.sum(outer_cos * real_sums + outer_sin * imag_sums, axis=-2) / period_f
    imag_coef = jnp.sum(outer_cos * imag_sums - outer_sin * real_sums, axis=-2) / period_f
    kept_mask = (2 * orders[None, :] < counts[:, None])[:, None, :]
    real_coef = jnp.where(kept_mask, real_coef, 0.0)
    imag_coef = jnp.where(kept_mask, imag_coef, 0.0)
    even_real = real_coef[:, :, :, 0] + real_coef[:, :, :, 1]
    even_imag = imag_coef[:, :, :, 0] + imag_coef[:, :, :, 1]
    odd_real = real_coef[:, :, :, 0] - real_coef[:, :, :, 1]
    odd_imag = imag_coef[:, :, :, 0] - imag_coef[:, :, :, 1]
    stacked = jnp.stack(
        [jnp.stack([even_real, even_imag], 2), jnp.stack([odd_real, odd_imag], 2)], 2
    )
    rounded = (weights[:, None] * stacked).astype(jnp.bfloat16)
    return jnp.swapaxes(rounded, 4, 5)


def synthesise(fourier_rows, counts, orders):
    fourier = jnp.swapaxes(fourier_rows, 4, 5)
    blocks = PPAD // 128
    cos_inner, sin_inner, cos_outer, sin_outer = fourier_tables(counts, orders, blocks)
    even_parts = fourier[:, :, 0].astype(jnp.float32)
    odd_parts = fourier[:, :, 1].astype(jnp.float32)
    hemispheres = jnp.stack([even_parts + odd_parts, even_parts - odd_parts], axis=3)
    kept_mask = 2 * orders[None, :] < counts[:, None]
    factor = jnp.where(orders == 0, 1.0, 2.0)
    hemispheres = jnp.where(kept_mask, hemispheres, 0.0) * factor
    real_hemisphere = jnp.moveaxis(hemispheres[:, :, 0], 3, 2)[..., None, :]
    imag_hemisphere = jnp.moveaxis(hemispheres[:, :, 1], 3, 2)[..., None, :]
    outer_cos = cos_outer[:, None]
    outer_sin = sin_outer[:, None]
    real_phase = outer_cos * real_hemisphere - outer_sin * imag_hemisphere
    imag_phase = outer_sin * real_hemisphere + outer_cos * imag_hemisphere
    stacked = jnp.concatenate([real_phase, imag_phase], axis=-1).astype(jnp.bfloat16)
    dft_table = jnp.concatenate([cos_inner, -sin_inner], axis=-1)
    values = jnp.einsum(
        "vlshbc,skc->vlshbk", stacked, dft_table, preferred_element_type=jnp.float32
    )
    flattened = values.reshape(values.shape[:4] + (PPAD,))
    inside = jnp.arange(PPAD)[None, :] < counts[:, None]
    return jnp.where(inside[:, None, :], flattened, 0.0).astype(jnp.bfloat16)


def add_terms(earlier, later):
    return earlier + later


def on_device(grid_field, coupling, points, lat_ids, wn_ids):
    orders, all_slots = (
        lax.all_gather(wn_ids, "band", axis=0, tiled=True),
        lax.all_gather(lat_ids, "band", axis=0, tiled=True),
    )
    counts = jnp.take(points, lat_ids)
    local_cos, local_sin = latitude_angles(lat_ids)
    weights = math.pi / (2.0 * NH) * local_sin
    coeffs = analyse(grid_field, counts, orders, weights)
    received = lax.all_to_all(coeffs, "band", split_axis=4, concat_axis=5, tiled=True)
    all_cos, all_sin = latitude_angles(all_slots)
    legendre_table = legendre_rows(wn_ids, all_cos, all_sin)
    spectral = jnp.einsum(
        "vlprmi,qpmi->vlprmq", received, legendre_table, preferred_element_type=jnp.float32
    )
    weighted = coupling[:, :, None, None, None, None] * spectral
    running = jnp.cumsum(weighted, axis=1)
    level_total = running[:, -1]
    earlier = carried_in(level_total, "fld", add_terms, jnp.zeros_like(level_total))
    damping_rows = jnp.transpose(damping(wn_ids), (1, 2, 0))[None, None, :, None, :, :]
    updated = (damping_rows * (spectral + earlier[:, None] + running - weighted)).astype(
        jnp.bfloat16
    )
    outgoing = jnp.einsum(
        "vlprmq,qpmi->vlprmi", updated, legendre_table, preferred_element_type=jnp.float32
    ).astype(jnp.bfloat16)
    fourier = lax.all_to_all(outgoing, "band", split_axis=5, concat_axis=4, tiled=True)
    return synthesise(fourier, counts, orders)


def solution(mesh):
    in_specs = (P(None, "fld", "band", None, None), P(None, "fld"), P(), P("band"), P("band"))
    out_specs = P(None, "fld", "band", None, None)
    return jax.shard_map(
        on_device, mesh=mesh, in_specs=in_specs, out_specs=out_specs, check_vma=False
    )
```

profile of v0, /device:TPU:0, one launch (start us, length us, event | category | flops | bytes accessed | tf_op | source)
XLA Modules:
  0.0 945.1 jit_solution(17061320564376272332)
XLA Ops:
  0.7 1.1 gather_fusion
  2.6 1.2 dynamic-slice
  6.8 14.1 %all-reduce.2 = (s32[1280]{0:T(1024)S(1)}, s32[128]{0:T(128)S(1)}) all-reduce(s32[1280]{0:T(1024)S(1)} %dynamic-update-slice.1, s32[128]{0:T(128)S(1)} %dynamic-update-slice), channel_id=1, replica_groups=mesh['band'=16,'fld'=2] {'band'}, use_global_device_ids=true, to_apply=%add.1 | all-reduce | flops 1408 | bytes 11264
  21.0 68.9 %cosine_convert_fusion = bf16[80,128,128]{2,1,0:T(8,128)(2,1)} fusion(f32[80]{0:T(128)S(1)} %convert_element_type.160, pred[80]{0:T(512)(128)(4,1)S(1)} %compare_bitcast_fusion, s32[80]{0:T(128)S(1)} %get-tuple-element.179, s32[128,128]{1,0:T(8,128)S(1)} %multiply_bitcast_fusion), kind=kLoop, calls=%fused_computation.156 | loop fusion | flops 14417920 | bytes 2687696 | tf_op jit(solution)/shard_map/convert_element_type | solution.py:89
  89.8 69.3 %fusion.73 = bf16[80,128,128]{2,1,0:T(8,128)(2,1)} fusion(f32[80]{0:T(128)S(1)} %convert_element_type.160, pred[80]{0:T(512)(128)(4,1)S(1)} %compare_bitcast_fusion, s32[80]{0:T(128)S(1)} %get-tuple-element.179, s32[128,128]{1,0:T(8,128)S(1)} %multiply_bitcast_fusion), kind=kLoop, calls=%fused_computation.163 | loop fusion | flops 18350080 | bytes 2687696 | tf_op jit(solution)/shard_map/neg | solution.py:145
  159.5 7.6 copy_select_fusion.1
  167.1 11.7 %reshape.556 = bf16[2,2,80,2,41,128]{5,4,2,3,1,0:T(8,128)(2,1)} reshape(bf16[2,2,80,2,5248]{4,2,3,1,0:T(8,128)(2,1)} %copy_select_fusion.1) | data formatting | bytes 13434880 | tf_op jit(solution)/shard_map/reshape | solution.py:102
  178.9 27.8 %fusion.90 = (f32[80,41,128]{2,1,0:T(8,128)S(1)}, f32[80,41,128]{2,1,0:T(8,128)}) fusion(f32[80]{0:T(128)S(1)} %convert_element_type.160, pred[80]{0:T(512)(128)(4,1)S(1)} %compare_bitcast_fusion, s32[80]{0:T(128)S(1)} %get-tuple-element.179, s32[41,128]{1,0:T(8,128)S(1)} %multiply_bitcast_fusion.1), kind=kLoop, calls=%fused_computation.176 | loop fusion | flops 4198400 | bytes 3380432 | tf_op jit(solution)/shard_map/cos | solution.py:91
  206.8 15.3 %convolution_bitcast_fusion = f32[2,2,80,2,41,256]{5,4,3,1,0,2:T(8,128)} fusion(bf16[2,2,80,2,41,128]{5,4,2,3,1,0:T(8,128)(2,1)} %reshape.556, bf16[80,128,128]{2,1,0:T(8,128)(2,1)} %fusion.73, bf16[80,128,128]{2,1,0:T(8,128)(2,1)} %cosine_convert_fusion), kind=kOutput, calls=%fused_computation.143 | convolution fusion | flops 1730150400 | bytes 38830080 | tf_op jit(solution)/shard_map/vlshbk,skc->vlshbc/dot_general | solution.py:104
  222.1 13.3 %add_reduce_fusion = (f32[2,2,80,2,128]{4,3,1,0,2:T(2,128)S(1)}, f32[2,2,80,2,128]{4,3,1,0,2:T(2,128)S(1)}) fusion(f32[2,2,80,2,41,256]{5,4,3,1,0,2:T(8,128)} %convolution_bitcast_fusion, f32[80,41,128]{2,1,0:T(8,128)} %get-tuple-element.226, f32[80,41,128]{2,1,0:T(8,128)S(1)} %get-tuple-element.225), kind=kLoop, calls=%fused_computation.140 | loop fusion | flops 26705920 | bytes 30883840 | tf_op jit(solution)/shard_map/reduce_sum | solution.py:112
  237.1 2.0 copy.124
  239.1 3.7 all-to-all-start
  243.4 1.1 copy.112
  245.6 2.0 copy.114
  247.6 524.3 %while.28 = (s32[]{:T(128)}, f32[8,1280]{1,0:T(8,128)S(1)}, f32[8,1280]{1,0:T(8,128)S(1)}, f32[8,1280]{1,0:T(8,128)S(1)}, bf16[160,8,8,1280]{3,2,1,0:T(8,128)(2,...) while((s32[]{:T(128)}, f32[8,1280]{1,0:T(8,128)S(1)}, ...), condition=%wide.region_2.5_spmd.clone, body=%wide.region_1.4_spmd.clone.sunk | while | flops 2754569 | bytes 1978075 | solution.py:70
  772.3 1.6 all_to_all.29
  773.9 22.5 %fusion.85 = f32[2,2,2,2,8,640]{5,3,1,0,4,2:T(2,128)S(1)} fusion(bf16[2,2,2,2,8,1280]{5,3,1,0,4,2:T(2,128)(2,1)} %all_to_all.29, bf16[640,2,8,1280,1,1]{3,2,1,0,5,4:T(8,128)(2,1)} %bitcast.216), kind=kOutput, calls=%fused_computation.172 | convolution fusion | flops 209715200 | bytes 26869760 | tf_op jit(solution)/shard_map/vlprmi,qpmi->vlprmq/dot_general | solution.py:170
  796.7 5.4 all-gather
  802.2 18.4 %fusion.77 = bf16[2,2,2,2,8,1280]{5,3,1,0,4,2:T(2,128)(2,1)} fusion(bf16[640,2,8,1280,1,1]{3,2,1,0,5,4:T(8,128)(2,1)} %bitcast.217, f32[2,2,2,2,8,640]{5,3,1,0,4,2:T(2,128)S(1)} %fusion.96, f32[2,2,2,2,8,640]{5,3,1,0,4,2:T(2,128)S(1)} %fusion.85, f32[2,2,2,8,640]{4,2,0,3,1:T(2,128)S(1)} %copy.129, f32[2,2]{1,0:T(2,128)S(1)} %copy-done.2, ...), kind=kOutput, calls=%fused_computation.165 | convolution fusion | flops 210370560 | bytes 27402256 | tf_op jit(solution)/shard_map/vlprmq,qpmi->vlprmi/dot_general | solution.py:181
  820.6 10.4 %copy.131 = bf16[2,2,2,2,8,1280]{4,3,2,1,0,5:T(2,128)(2,1)} copy(bf16[2,2,2,2,8,1280]{5,3,1,0,4,2:T(2,128)(2,1)} %fusion.77) | data formatting | bytes 655360 | tf_op jit(solution)/shard_map/convert_element_type | solution.py:183
  831.0 15.5 %reshape.584 = bf16[16,2,5120]{2,1,0:T(2,128)(2,1)} reshape(bf16[1280,2,2,2,2,8]{5,4,3,2,1,0:T(2,128)(2,1)} %bitcast.206) | data formatting | bytes 655360
  846.5 6.1 all-to-all-start.1
  852.7 10.9 %all-to-all-done.1 = bf16[16,2,5120]{2,1,0:T(2,128)(2,1)S(1)} async-done(((bf16[16,2,5120]{2,1,0:T(2,128)(2,1)}), bf16[16,2,5120]{2,1,0:T(2,128)(2,1)S(1)}, u32[]{:S(2)}, u32[]{:S(2)}) %all-to-all-start.1) | async-done | bytes 327712 | tf_op jit(solution)/shard_map/all_to_all | solution.py:184
  863.6 7.2 reshape.585
  870.8 9.5 %copy.132 = bf16[2,2,2,2,8,16,80]{6,4,5,3,2,1,0:T(8,128)(2,1)S(1)} copy(bf16[2,2,2,2,8,16,80]{4,3,2,1,0,6,5:T(2,128)(2,1)} %bitcast.204) | data formatting | bytes 655360 | tf_op jit(solution)/shard_map/all_to_all | solution.py:184
  880.3 10.6 %copy.147 = bf16[2,2,2,2,8,16,80]{6,4,5,3,1,0,2:T(8,128)(2,1)} copy(bf16[2,2,2,2,8,16,80]{4,3,2,1,0,6,5:T(2,128)(2,1)} %bitcast.205) | data formatting | bytes 655360 | tf_op jit(solution)/shard_map/transpose | solution.py:129
  894.0 1.3 copy.136
  896.2 8.6 subtract_convert_fusion
  904.8 11.2 %fusion.64 = bf16[2,2,80,2,41,128]{5,4,3,1,0,2:T(8,128)(2,1)} fusion(bf16[2,2,80,2,41,128]{5,4,3,1,0,2:T(8,128)(2,1)} %get-tuple-element.217, bf16[2,2,80,2,41,128]{5,4,3,1,0,2:T(8,128)(2,1)} %get-tuple-element.216, bf16[80,128,128]{2,1,0:T(8,128)(2,1)} %fusion.73, bf16[80,128,128]{2,1,0:T(8,128)(2,1)} %cosine_convert_fusion), kind=kOutput, calls=%fused_computation.148 | convolution fusion | flops 1757020160 | bytes 25395200 | tf_op jit(solution)/shard_map/vlshbc,skc->vlshbk/dot_general | solution.py:146
  916.0 14.4 %reshape.582 = bf16[2,2,80,2,5248]{4,3,1,0,2:T(2,128)(2,1)} reshape(bf16[2,2,80,2,41,128]{5,4,3,1,0,2:T(8,128)(2,1)} %fusion.64) | data formatting | bytes 13434880 | tf_op jit(solution)/shard_map/reshape | solution.py:149
  930.5 4.1 fusion.63
  934.6 10.1 %copy.139 = bf16[2,2,80,2,5248]{4,3,2,1,0:T(2,128)(2,1)} copy(bf16[2,2,80,2,5248]{4,2,3,1,0:T(8,128)(2,1)S(1)} %fusion.63) | data formatting | bytes 13434880 | tf_op jit(solution)/shard_map/convert_element_type | solution.py:151
  (2147 shorter events, 527.9 us)
Async XLA Ops:
  0.0 0.7 copy-start
  0.0 159.5 %copy-start.3 = (s32[80]{0:T(128)S(1)}, s32[80]{0:T(128)}, u32[]{:S(2)}) copy-start(s32[80]{0:T(128)} %param.16) | copy-start | bytes 964
  235.4 7.4 copy-start.4
  239.1 533.0 %all-to-all-start = ((bf16[2,2,2,2,128,80]{5,3,2,1,0,4:T(2,128)(2,1)}), bf16[2,2,2,2,128,80]{5,3,2,1,0,4:T(2,128)(2,1)S(1)}, u32[]{:S(2)}, u32[]{:S(2)}) async-start(bf16[2,2,2,2,128,80]{5,3,2,1,0,4:T(2,128)(2,1)} %copy.124), calls=%async_computation | async-start | bytes 1048576 | tf_op jit(solution)/shard_map/all_to_all | solution.py:167
  773.9 22.6 %copy-start.2 = (f32[2,2]{1,0:T(2,128)S(1)}, f32[2,2]{1,0:T(2,128)}, u32[]{:S(2)}) copy-start(f32[2,2]{1,0:T(2,128)} %param.14) | copy-start | bytes 52
  846.5 17.1 %all-to-all-start.1 = ((bf16[16,2,5120]{2,1,0:T(2,128)(2,1)}), bf16[16,2,5120]{2,1,0:T(2,128)(2,1)S(1)}, u32[]{:S(2)}, u32[]{:S(2)}) async-start(bf16[16,2,5120]{2,1,0:T(2,128)(2,1)} %reshape.584), calls=%async_computation.1 | async-start | bytes 655360 | tf_op jit(solution)/shard_map/all_to_all | solution.py:184
  930.4 14.2 %copy-start.1 = (s32[1280]{0:T(1024)S(1)}, s32[1280]{0:T(1024)}, u32[]{:S(2)}) copy-start(s32[1280]{0:T(1024)} %param.15) | copy-start | bytes 15364
where the time goes:
time: 957 us; the launch traced here: 945 us
  local copies, waits for them, and re-layouts  458 us (48%)
  other arithmetic  370 us (39%)
  matrix products  67.4 us (7%)
  blocking collectives  19.5 us (2%)
  waiting for transfers between devices  10.9 us (1%)
  starting transfers between devices  9.8 us (1%)
    mul x160, local copies, waits for them, and re-layouts, advance(): newest = factor * (cosine_row * current - backward * previous)  128 us
    while x1120, other arithmetic  119 us
    broadcast_in_dim x160, local copies, waits for them, and re-layouts, advance(): jnp.where(inside, current * jnp.exp(running_log), 0.0).astype(jnp.bfloat16)  115 us
    dynamic_update_slice x160, local copies, waits for them, and re-layouts, legendre_rows(): lax.scan(advance, (start_row, jnp.zeros_like(start_row), scaled_log), (fa...  109 us
    neg x1, other arithmetic, synthesise(): dft_table = jnp.concatenate([cos_inner, -sin_inner], axis=-1)  69.3 us
    convert_element_type x1, other arithmetic, fourier_tables(): jnp.cos(inner_angle).astype(jnp.bfloat16)  68.9 us
    unnamed x20, local copies, waits for them, and re-layouts  29.8 us
    cos x1, other arithmetic, fourier_tables(): jnp.cos(block_angle)  27.8 us
  transfers between devices with their start and end apart: 2, of which 1 were waited for; matrix products, arithmetic and copies ran while one was open for 55% of the time, Pallas kernels for 0%

commit v1 on v0

--- a/solution.py
+++ b/solution.py
@@ -181,7 +181,10 @@
     outgoing = jnp.einsum(
         "vlprmq,qpmi->vlprmi", updated, legendre_table, preferred_element_type=jnp.float32
     ).astype(jnp.bfloat16)
-    fourier = lax.all_to_all(outgoing, "band", split_axis=5, concat_axis=4, tiled=True)
+    fourier = jnp.concatenate(
+        lax.all_to_all(jnp.stack(jnp.split(outgoing, lax.axis_size("band"), axis=5)), "band", 0, 0),
+        axis=4,
+    )
     return synthesise(fourier, counts, orders)
 
 

time: 957 us -> 908 us (0.949)
  local copies, waits for them, and re-layouts: 458 us -> 404 us
    unnamed x20 -> x35, local copies, waits for them, and re-layouts: 29.8 us -> 18.1 us
    transpose x1, local copies, waits for them, and re-layouts: 10.6 us -> 0.1 us  [synthesise(): fourier = jnp.swapaxes(fourier_rows, 4, 5)]
    convert_element_type x1 -> x0, local copies, waits for them, and re-layouts: 10.4 us -> none  [on_device(): outgoing = jnp.einsum('vlprmq,qpmi->vlprmi', updated, legendre_table, pre...]
  transfers between devices with their start and end apart: 2 -> 2, of which waited for: 1 -> 1; matrix products, arithmetic and copies ran while one was open for 55% -> 57% of each run, Pallas kernels for 0% -> 0%
where the time goes in v1:
time: 908 us; the launch traced here: 897 us
  local copies, waits for them, and re-layouts  404 us (44%)
  other arithmetic  368 us (41%)
  matrix products  71.7 us (8%)
  blocking collectives  19.5 us (2%)
  waiting for transfers between devices  14.1 us (2%)
  starting transfers between devices  9.81 us (1%)
    while x1120, other arithmetic  119 us
    mul x160, local copies, waits for them, and re-layouts, advance(): newest = factor * (cosine_row * current - backward * previous)  119 us
    broadcast_in_dim x160, local copies, waits for them, and re-layouts, advance(): jnp.where(inside, current * jnp.exp(running_log), 0.0).astype(jnp.bfloat16)  115 us
    dynamic_update_slice x160, local copies, waits for them, and re-layouts, legendre_rows(): lax.scan(advance, (start_row, jnp.zeros_like(start_row), scaled_log), (fa...  109 us
    neg x1, other arithmetic, synthesise(): dft_table = jnp.concatenate([cos_inner, -sin_inner], axis=-1)  69.4 us
    convert_element_type x1, other arithmetic, fourier_tables(): jnp.cos(inner_angle).astype(jnp.bfloat16)  68.9 us
    cos x1, other arithmetic, fourier_tables(): jnp.cos(block_angle)  27.8 us
    dot_general x1, matrix products, on_device(): jnp.einsum('vlprmq,qpmi->vlprmi', updated, legendre_table, preferred_elem...  22.7 us
  transfers between devices with their start and end apart: 2, of which 1 were waited for; matrix products, arithmetic and copies ran while one was open for 57% of the time, Pallas kernels for 0%

profile of v1, /device:TPU:0, one launch (start us, length us, event | category | flops | bytes accessed | tf_op | source)
XLA Modules:
  0.0 897.1 jit_solution(575597854247605540)
XLA Ops:
  0.7 1.1 gather_fusion
  2.6 1.2 dynamic-slice
  5.1 0.9 dynamic-update-slice.1
  6.0 0.8 dynamic-update-slice
  6.8 14.1 %all-reduce.2 = (s32[1280]{0:T(1024)S(1)}, s32[128]{0:T(128)S(1)}) all-reduce(s32[1280]{0:T(1024)S(1)} %dynamic-update-slice.1, s32[128]{0:T(128)S(1)} %dynamic-update-slice), channel_id=1, replica_groups=mesh['band'=16,'fld'=2] {'band'}, use_global_device_ids=true, to_apply=%add.1 | all-reduce | flops 1408 | bytes 11264
  21.0 68.9 %cosine_convert_fusion = bf16[80,128,128]{2,1,0:T(8,128)(2,1)} fusion(f32[80]{0:T(128)S(1)} %convert_element_type.160, pred[80]{0:T(512)(128)(4,1)S(1)} %compare_bitcast_fusion, s32[80]{0:T(128)S(1)} %get-tuple-element.175, s32[128,128]{1,0:T(8,128)S(1)} %multiply_bitcast_fusion), kind=kLoop, calls=%fused_computation.156 | loop fusion | flops 14417920 | bytes 2687696 | tf_op jit(solution)/shard_map/convert_element_type | solution.py:89
  89.8 69.4 %fusion.73 = bf16[80,128,128]{2,1,0:T(8,128)(2,1)} fusion(f32[80]{0:T(128)S(1)} %convert_element_type.160, pred[80]{0:T(512)(128)(4,1)S(1)} %compare_bitcast_fusion, s32[80]{0:T(128)S(1)} %get-tuple-element.175, s32[128,128]{1,0:T(8,128)S(1)} %multiply_bitcast_fusion), kind=kLoop, calls=%fused_computation.163 | loop fusion | flops 18350080 | bytes 2687696 | tf_op jit(solution)/shard_map/neg | solution.py:145
  159.6 7.6 copy_select_fusion.1
  167.2 11.7 %reshape.562 = bf16[2,2,80,2,41,128]{5,4,2,3,1,0:T(8,128)(2,1)} reshape(bf16[2,2,80,2,5248]{4,2,3,1,0:T(8,128)(2,1)} %copy_select_fusion.1) | data formatting | bytes 13434880 | tf_op jit(solution)/shard_map/reshape | solution.py:102
  178.9 27.8 %fusion.90 = (f32[80,41,128]{2,1,0:T(8,128)S(1)}, f32[80,41,128]{2,1,0:T(8,128)}) fusion(f32[80]{0:T(128)S(1)} %convert_element_type.160, pred[80]{0:T(512)(128)(4,1)S(1)} %compare_bitcast_fusion, s32[80]{0:T(128)S(1)} %get-tuple-element.175, s32[41,128]{1,0:T(8,128)S(1)} %multiply_bitcast_fusion.1), kind=kLoop, calls=%fused_computation.176 | loop fusion | flops 4198400 | bytes 3380432 | tf_op jit(solution)/shard_map/cos | solution.py:91
  206.8 15.3 %convolution_bitcast_fusion = f32[2,2,80,2,41,256]{5,4,3,1,0,2:T(8,128)} fusion(bf16[2,2,80,2,41,128]{5,4,2,3,1,0:T(8,128)(2,1)} %reshape.562, bf16[80,128,128]{2,1,0:T(8,128)(2,1)} %fusion.73, bf16[80,128,128]{2,1,0:T(8,128)(2,1)} %cosine_convert_fusion), kind=kOutput, calls=%fused_computation.143 | convolution fusion | flops 1730150400 | bytes 38830080 | tf_op jit(solution)/shard_map/vlshbk,skc->vlshbc/dot_general | solution.py:104
  222.1 13.3 %add_reduce_fusion = (f32[2,2,80,2,128]{4,3,1,0,2:T(2,128)S(1)}, f32[2,2,80,2,128]{4,3,1,0,2:T(2,128)S(1)}) fusion(f32[2,2,80,2,41,256]{5,4,3,1,0,2:T(8,128)} %convolution_bitcast_fusion, f32[80,41,128]{2,1,0:T(8,128)} %get-tuple-element.222, f32[80,41,128]{2,1,0:T(8,128)S(1)} %get-tuple-element.221), kind=kLoop, calls=%fused_computation.140 | loop fusion | flops 26705920 | bytes 30883840 | tf_op jit(solution)/shard_map/reduce_sum | solution.py:112
  237.1 2.0 copy.95
  239.1 3.7 all-to-all-start
  243.4 1.1 copy.83
  244.5 1.1 copy.84
  245.6 2.0 copy.85
  247.7 513.7 %while.28 = (s32[]{:T(128)}, f32[8,1280]{1,0:T(8,128)S(1)}, f32[8,1280]{1,0:T(8,128)S(1)}, f32[8,1280]{1,0:T(8,128)S(1)}, bf16[160,8,8,1280]{3,2,1,0:T(8,128)(2,...) while((s32[]{:T(128)}, f32[8,1280]{1,0:T(8,128)S(1)}, ...), condition=%wide.region_2.5_spmd.clone, body=%wide.region_1.4_spmd.clone.sunk | while | flops 2754569 | bytes 1978075 | solution.py:70
  476.4 0.8 fusion.146
  710.7 0.8 fusion.146
  761.8 1.6 all_to_all.19
  763.3 22.5 %fusion.85 = f32[2,2,2,2,8,640]{5,3,1,0,4,2:T(2,128)S(1)} fusion(bf16[2,2,2,2,8,1280]{5,3,1,0,4,2:T(2,128)(2,1)} %all_to_all.19, bf16[640,2,8,1280,1,1]{3,2,1,0,5,4:T(8,128)(2,1)} %bitcast.279), kind=kOutput, calls=%fused_computation.172 | convolution fusion | flops 209715200 | bytes 26869760 | tf_op jit(solution)/shard_map/vlprmi,qpmi->vlprmq/dot_general | solution.py:170
  786.6 5.4 all-gather
  792.1 22.7 %fusion.77 = bf16[2,2,2,2,8,1280]{5,3,1,0,4,2:T(2,128)(2,1)S(1)} fusion(bf16[640,2,8,1280,1,1]{3,2,1,0,5,4:T(8,128)(2,1)} %bitcast.280, f32[2,2,2,2,8,640]{5,3,1,0,4,2:T(2,128)S(1)} %fusion.96, f32[2,2,2,2,8,640]{5,3,1,0,4,2:T(2,128)} %copy-done.2, f32[2,2,2,8,640]{4,2,0,3,1:T(2,128)S(1)} %copy.100, f32[2,2]{1,0:T(2,128)S(1)} %copy-done.3, ...), kind=kOutput, calls=%fused_computation.165 | convolution fusion | flops 210370560 | bytes 27402256 | tf_op jit(solution)/shard_map/vlprmq,qpmi->vlprmi/dot_general | solution.py:181
  826.0 6.1 all-to-all-start.1
  832.2 14.1 %all-to-all-done.1 = bf16[16,2,2,2,2,8,80]{6,4,2,1,5,3,0:T(2,128)(2,1)S(1)} async-done(((bf16[16,2,2,2,2,8,80]{6,4,2,1,5,3,0:T(2,128)(2,1)}), bf16[16,2,2,2,2,8,80]{6,4,2,1,5,3,0:T(2,128)(2,1)S(1)}, u32[]{:S(2)}, u32[]{:S(2)}) %all-to-all-start.1) | async-done | bytes 327712 | tf_op jit(solution)/shard_map/all_to_all | solution.py:185
  847.0 0.9 copy.106
  848.1 8.7 subtract_convert_fusion
  856.8 11.2 %fusion.64 = bf16[2,2,80,2,41,128]{5,4,3,1,0,2:T(8,128)(2,1)} fusion(bf16[2,2,80,2,41,128]{5,4,3,1,0,2:T(8,128)(2,1)} %get-tuple-element.213, bf16[2,2,80,2,41,128]{5,4,3,1,0,2:T(8,128)(2,1)} %get-tuple-element.212, bf16[80,128,128]{2,1,0:T(8,128)(2,1)} %fusion.73, bf16[80,128,128]{2,1,0:T(8,128)(2,1)} %cosine_convert_fusion), kind=kOutput, calls=%fused_computation.148 | convolution fusion | flops 1757020160 | bytes 25395200 | tf_op jit(solution)/shard_map/vlshbc,skc->vlshbk/dot_general | solution.py:146
  868.0 14.4 %reshape.590 = bf16[2,2,80,2,5248]{4,3,1,0,2:T(2,128)(2,1)} reshape(bf16[2,2,80,2,41,128]{5,4,3,1,0,2:T(8,128)(2,1)} %fusion.64) | data formatting | bytes 13434880 | tf_op jit(solution)/shard_map/reshape | solution.py:149
  882.5 4.1 fusion.63
  886.6 10.1 %copy.109 = bf16[2,2,80,2,5248]{4,3,2,1,0:T(2,128)(2,1)} copy(bf16[2,2,80,2,5248]{4,2,3,1,0:T(8,128)(2,1)S(1)} %fusion.63) | data formatting | bytes 13434880 | tf_op jit(solution)/shard_map/convert_element_type | solution.py:151
  (2162 shorter events, 521.6 us)
Async XLA Ops:
  0.0 0.7 copy-start
  0.0 159.5 %copy-start.4 = (s32[80]{0:T(128)S(1)}, s32[80]{0:T(128)}, u32[]{:S(2)}) copy-start(s32[80]{0:T(128)} %param.16) | copy-start | bytes 964
  235.4 7.4 copy-start.5
  239.1 522.4 %all-to-all-start = ((bf16[2,2,2,2,128,80]{5,3,2,1,0,4:T(2,128)(2,1)}), bf16[2,2,2,2,128,80]{5,3,2,1,0,4:T(2,128)(2,1)S(1)}, u32[]{:S(2)}, u32[]{:S(2)}) async-start(bf16[2,2,2,2,128,80]{5,3,2,1,0,4:T(2,128)(2,1)} %copy.95), calls=%async_computation | async-start | bytes 1048576 | tf_op jit(solution)/shard_map/all_to_all | solution.py:167
  763.3 22.5 %copy-start.3 = (f32[2,2]{1,0:T(2,128)S(1)}, f32[2,2]{1,0:T(2,128)}, u32[]{:S(2)}) copy-start(f32[2,2]{1,0:T(2,128)} %param.14) | copy-start | bytes 52
  785.8 0.7 copy-start.2
  826.0 20.3 %all-to-all-start.1 = ((bf16[16,2,2,2,2,8,80]{6,4,2,1,5,3,0:T(2,128)(2,1)}), bf16[16,2,2,2,2,8,80]{6,4,2,1,5,3,0:T(2,128)(2,1)S(1)}, u32[]{:S(2)}, u32[]{:S(2)}) async-start(bf16[16,2,2,2,2,8,80]{6,4,2,1,5,3,0:T(2,128)(2,1)} %fusion.116), calls=%async_computation.1 | async-start | bytes 1048576 | tf_op jit(solution)/shard_map/all_to_all | solution.py:185
  882.4 14.2 %copy-start.1 = (s32[1280]{0:T(1024)S(1)}, s32[1280]{0:T(1024)}, u32[]{:S(2)}) copy-start(s32[1280]{0:T(1024)} %param.15) | copy-start | bytes 15364
